TPU v7x, 32 devices: a whole 2x2x4 slice. The times are simulated.
32 devices in a mesh: mem: 4 (over y, x), lat: 8 (over z, core).
Axes of the slice: x: 2, y: 2, z: 4, core: 2. Of those that a mesh axis runs over, the one named last changes fastest.
Arguments:
- controls: float32 [24, 16, 8, 96], P('mem', None, 'lat'), may hold values from -6 to 6
- perturbations: bfloat16 [24, 64, 32, 384], P('mem', None, 'lat'), may hold values from -1.25 to 1.25
- precision_weight: bfloat16 [64, 128, 1536], P(None, 'lat'), may hold values from 0.25 to 4
- north_coef: float32 [128, 1536], P('lat'), may hold values from 0.02 to 0.24
- east_coef: float32 [128, 1536], P('lat'), may hold values from 0.02 to 0.24
- fine_source: int32 [128], P('lat'), may hold values from 0 to 30, as said below
- fine_frac: float32 [128], P('lat'), may hold values from 0 to 1
Outputs:
- gradient: float32 [24, 16, 8, 96], P('mem', None, 'lat')
Inputs may be any that keep to these rules, and one draw needn't show every extreme that they name: Fine row f lies in band b = f // 16; its source rows fine_source[f] and fine_source[f] + 1 satisfy max(b * 4 - 4, 0) <= fine_source[f] <= min((b + 1) * 4 + 2, 30), and both ends are reached in every band.
All inputs are finite; a program needn't handle non-finite values.
Results may differ from a plain program's by a relative error of at most 0.0003.
Values sent between devices are 32-bit elements; how exact they have to be, the bound alone decides.
A program may use at most 128 MiB of HBM per device.

v0:
```python
import functools
import jax
import jax.numpy as jnp
import numpy as np
from jax import lax
from jax.experimental import pallas as pl
from jax.experimental.pallas import tpu as pltpu
from jax.sharding import PartitionSpec as P

PASSES = 5
REACH = 4
LANES = 128
F32 = jnp.float32
BF16 = jnp.bfloat16
MESH = pl.DeviceIdType.MESH


def refine_matrix(count, mode):
    weights = [(0.375, 0.625, 0.0), (0.125, 0.875, 0.0), (0.0, 0.875, 0.125), (0.0, 0.625, 0.375)]
    full = np.zeros((4 * count, count + 2), np.float32)
    for q in range(count):
        for r in range(4):
            full[4 * q + r, q : q + 3] += weights[r]
    if mode == "pad":
        return full
    inner = full[:, 1:-1].copy()
    if mode == "edge":
        inner[:, 0] += full[:, 0]
        inner[:, -1] += full[:, -1]
    else:
        inner[:, -1] += full[:, 0]
        inner[:, 0] += full[:, -1]
    return inner


def split3(value):
    high = value.astype(BF16)
    rest = value - high.astype(F32)
    mid = rest.astype(BF16)
    low = (rest - mid.astype(F32)).astype(BF16)
    return high, mid, low


def dot(a, b):
    return jnp.dot(a, b, preferred_element_type=F32)


def kernel(
    dims,
    ctl_ref, pert_hbm, pw_hbm, north_ref, east_ref, sf_ref, up_ref, lon_ref, down_ref, lont_ref,
    out_ref,
    ctl, pert, pw, wrows, co, sfr, ls, mids, rsr, midx, fld, blend, contrib, adjr, fa, gp, gpr, wown,
    local_sem, send_sem, recv_sem,
):
    nm, nl, mb, cl, cw, lv, mr, mw, fr, fw = dims
    lp = lv // nm
    h1, h2 = 2 * PASSES, PASSES
    ext = fr + 2 * h1
    mem, lat = lax.axis_index("mem"), lax.axis_index("lat")
    first, last = lat == 0, lat == nl - 1
    blocks = lp // 8

    cp_pert = pltpu.make_async_copy(pert_hbm, pert, local_sem.at[0])
    cp_pert.start()
    cp_pw = pltpu.make_async_copy(
        pw_hbm.at[pl.ds(mem * lp, lp)], pw, local_sem.at[1]
    )
    cp_pw.start()

    barrier = pltpu.get_barrier_semaphore()
    for step in (1, 2):
        @pl.when(lat >= step)
        def _():
            pl.semaphore_signal(barrier, inc=1, device_id={"lat": lat - step}, device_id_type=MESH)

        @pl.when(lat < nl - step)
        def _():
            pl.semaphore_signal(barrier, inc=1, device_id={"lat": lat + step}, device_id_type=MESH)
    for k in range(1, nm):
        pl.semaphore_signal(
            barrier, inc=1, device_id={"mem": lax.rem(mem + k, nm)}, device_id_type=MESH
        )
    present = nm - 1
    for step in (1, 2):
        present = present + (lat >= step).astype(jnp.int32) + (lat < nl - step).astype(jnp.int32)
    pl.semaphore_wait(barrier, present)

    def lat_copy(slot, step, src, dst):
        copy = pltpu.make_async_remote_copy(
            src_ref=src, dst_ref=dst, send_sem=send_sem.at[slot], recv_sem=recv_sem.at[slot],
            device_id={"lat": lat + step}, device_id_type=MESH,
        )
        if step > 0:
            return copy, lat < nl - step, lat >= step
        return copy, lat >= -step, lat < nl + step

    def start(item):
        copy, sends, _ = item

        @pl.when(sends)
        def _():
            copy.start()

    def wait_recv(item):
        copy, _, receives = item

        @pl.when(receives)
        def _():
            copy.wait_recv()

    def wait_send(item):
        copy, sends, _ = item

        @pl.when(sends)
        def _():
            copy.wait_send()

    pending = []

    c_up = lat_copy(0, 1, ctl_ref, ctl.at[0])
    c_dn = lat_copy(1, -1, ctl_ref, ctl.at[1])
    s_up = lat_copy(2, 1, sf_ref.at[pl.ds(fr - h1, h1)], sfr.at[pl.ds(0, h1)])
    s_dn = lat_copy(3, -1, sf_ref.at[pl.ds(0, h1)], sfr.at[pl.ds(h1, h1)])
    for item in (c_up, c_dn, s_up, s_dn):
        start(item)
        pending.append(item)

    rows_i = lax.broadcasted_iota(jnp.int32, (4 * LANES, 4 * LANES), 0)
    cols_i = lax.broadcasted_iota(jnp.int32, (4 * LANES, 4 * LANES), 1)
    perm = (rows_i == 4 * lax.rem(cols_i, LANES) + lax.div(cols_i, LANES)).astype(F32).astype(BF16)
    qblocks = mw // LANES

    for kind, ref in enumerate((north_ref, east_ref)):
        stacked = jnp.concatenate(split3(ref[...]), axis=0)
        for block in range(qblocks):
            moved = dot(stacked[:, block * 4 * LANES : (block + 1) * 4 * LANES], perm)
            exact = (moved[:fr] + moved[fr : 2 * fr]) + moved[2 * fr :]
            for phase in range(4):
                lanes = pl.ds(phase * mw + block * LANES, LANES)
                for row in range(fr):
                    co[h1 + row, kind : kind + 1, lanes] = exact[
                        row : row + 1, phase * LANES : (phase + 1) * LANES
                    ]
    k_up = lat_copy(4, 1, co.at[pl.ds(fr, h1)], co.at[pl.ds(0, h1)])
    k_dn = lat_copy(5, -1, co.at[pl.ds(h1, h1)], co.at[pl.ds(h1 + fr, h1)])
    for item in (k_up, k_dn):
        start(item)
        pending.append(item)

    wait_recv(c_up)
    wait_recv(c_dn)
    own = ctl_ref[...]
    below = jnp.where(first, own, ctl[0])
    above = jnp.where(last, own, ctl[1])
    lon = lon_ref[...]
    wide = []
    for part in (below, own, above):
        parts = split3(part.reshape(mb * cl, cw))
        wide.append(dot(parts[0], lon) + (dot(parts[1], lon) + dot(parts[2], lon)))
    cp_pert.wait()
    up3 = up_ref[...]
    for m in range(mb):
        stack = jnp.concatenate([w[m * cl : (m + 1) * cl] for w in wide], axis=0)
        raised = dot(up3, jnp.concatenate(split3(stack), axis=0))
        term = pert[m].astype(F32) * raised
        for t in range(qblocks):
            piece = term[:, t * LANES : (t + 1) * LANES]
            if m == 0:
                ls[t] = piece
            else:
                ls[t] += piece
    for r in range(mr):
        for t in range(qblocks):
            mids[r, :, t * LANES : (t + 1) * LANES] = ls[t, pl.ds(r, lv, stride=mr), :]

    rs = []
    for k in range(1, nm):
        target = lax.rem(mem + k, nm)
        copy = pltpu.make_async_remote_copy(
            src_ref=mids.at[:, pl.ds(pl.multiple_of(target * lp, 8), lp), :],
            dst_ref=rsr.at[k - 1],
            send_sem=send_sem.at[16 + k], recv_sem=recv_sem.at[16 + k],
            device_id={"mem": target}, device_id_type=MESH,
        )
        copy.start()
        rs.append(copy)

    cp_pw.wait()
    count = lp * fr
    to_i = lax.broadcasted_iota(jnp.int32, (count, count), 0)
    from_i = lax.broadcasted_iota(jnp.int32, (count, count), 1)
    turn = (from_i == lax.rem(to_i, lp) * fr + lax.div(to_i, lp)).astype(F32).astype(BF16)
    for block in range(qblocks):
        piece = pw[:, :, block * 4 * LANES : (block + 1) * 4 * LANES].reshape(count, 4 * LANES)
        turned = dot(turn, piece).astype(BF16)
        moved = dot(turned, perm)
        for phase in range(4):
            lanes = pl.ds(phase * mw + block * LANES, LANES)
            wown[:, :, lanes] = moved[:, phase * LANES : (phase + 1) * LANES].reshape(fr, lp, LANES)
    w_up = lat_copy(6, 1, wown.at[pl.ds(fr - h2, h2)], wrows.at[0])
    w_dn = lat_copy(7, -1, wown.at[pl.ds(0, h2)], wrows.at[1])
    for item in (w_up, w_dn):
        pending.append(item)

    mine = pl.ds(pl.multiple_of(mem * lp, 8), lp)
    total = mids[:, mine, :]
    for k in range(1, nm):
        rs[k - 1].wait_recv()
        total = total + rsr[k - 1]
    centre = 2 * mr
    midx[pl.ds(centre, mr)] = total
    near = []
    for slot, step in ((8, 1), (9, -1), (10, 2), (11, -2)):
        item = lat_copy(
            slot, step, midx.at[pl.ds(centre, mr)], midx.at[pl.ds(centre - step * mr, mr)]
        )
        start(item)
        pending.append(item)
        near.append(item)
    start(w_up)
    start(w_dn)

    zero_mid = jnp.zeros((mr, lp, mw), F32)
    for at, absent in ((1, first), (0, lat < 2), (3, last), (4, lat >= nl - 2)):
        @pl.when(absent)
        def _():
            midx[pl.ds(at * mr, mr)] = zero_mid

    @pl.when(first)
    def _():
        fld[h1 - 1] = jnp.zeros((lp, fw), F32)
        co[h1 - 1] = jnp.zeros((2, fw), F32)

    @pl.when(last)
    def _():
        fld[h1 + fr] = jnp.zeros((lp, fw), F32)

    for item in (s_up, s_dn, *near, k_up, k_dn):
        wait_recv(item)

    origin = (lat * mr - 2 * mr).astype(F32)

    def weight_of(source, fraction, r):
        place = source - origin
        lower = jnp.where(place == float(r), 1.0 - fraction, 0.0)
        return lower + jnp.where(place == float(r - 1), fraction, 0.0)

    def make_rows(ref, ref_row, ext_row, rows, base):
        def step(i, carry):
            source = jnp.broadcast_to(ref[ref_row + i, 0:1, :], (8, LANES))
            fraction = jnp.broadcast_to(ref[ref_row + i, 1:2, :], (8, LANES))
            weights = [weight_of(source, fraction, base + r) for r in range(3 * mr)]
            for b in range(blocks):
                levels = slice(8 * b, 8 * b + 8)
                pieces = []
                for t in range(qblocks):
                    value = weights[0] * midx[base, levels, t * LANES : (t + 1) * LANES]
                    for r in range(1, 3 * mr):
                        value = value + weights[r] * midx[
                            base + r, levels, t * LANES : (t + 1) * LANES
                        ]
                    pieces.append(value)
                row = jnp.concatenate(pieces, axis=1)
                before = pltpu.roll(row, 1, 1)
                after = pltpu.roll(row, mw - 1, 1)
                at = ext_row + i
                fld[at, levels, 0:mw] = 0.375 * before + 0.625 * row
                fld[at, levels, mw : 2 * mw] = 0.125 * before + 0.875 * row
                fld[at, levels, 2 * mw : 3 * mw] = 0.875 * row + 0.125 * after
                fld[at, levels, 3 * mw : 4 * mw] = 0.625 * row + 0.375 * after
            return carry

        lax.fori_loop(0, rows, step, 0)

    make_rows(sf_ref, 0, h1, fr, mr)

    @pl.when(jnp.logical_not(first))
    def _():
        make_rows(sfr, 0, 0, h1, 0)

    @pl.when(jnp.logical_not(last))
    def _():
        make_rows(sfr, h1, h1 + fr, h1, 2 * mr)

    def one_pass(low, high):
        for b in range(blocks):
            levels = slice(8 * b, 8 * b + 8)

            def phases(row):
                return [fld[row, levels, p * mw : (p + 1) * mw] for p in range(4)]

            def coef(row, kind, p):
                return co[row, kind : kind + 1, p * mw : (p + 1) * mw]

            centre0 = phases(low)
            under = phases(low - 1)
            flux0 = [coef(low - 1, 0, p) * (centre0[p] - under[p]) for p in range(4)]

            def step(row, carry):
                now, below_flux = carry
                over = phases(row + 1)
                east = [coef(row, 1, p) * (now[p + 1] - now[p]) for p in range(3)]
                east.append(coef(row, 1, 3) * (pltpu.roll(now[0], mw - 1, 1) - now[3]))
                west = [pltpu.roll(east[3], 1, 1)] + east[:3]
                north = [coef(row, 0, p) * (over[p] - now[p]) for p in range(4)]
                for p in range(4):
                    fld[row, levels, p * mw : (p + 1) * mw] = now[p] + (
                        (north[p] - below_flux[p]) + (east[p] - west[p])
                    )
                return over, north

            lax.fori_loop(low, high, step, (centre0, flux0))

    def smooth(margin):
        def body(p, carry):
            low = jnp.where(first, h1, margin + 1 + p)
            high = jnp.where(last, h1 + fr, ext - margin - 1 - p)
            one_pass(low, high)
            return carry

        lax.fori_loop(0, PASSES, body, 0)

    smooth(0)
    wait_recv(w_up)
    wait_recv(w_dn)

    def apply_own(i, carry):
        fld[h1 + i] = fld[h1 + i] * wown[i]
        return carry

    lax.fori_loop(0, fr, apply_own, 0)

    @pl.when(jnp.logical_not(first))
    def _():
        for i in range(h2):
            fld[h1 - h2 + i] = fld[h1 - h2 + i] * wrows[0, i]

    @pl.when(jnp.logical_not(last))
    def _():
        for i in range(h2):
            fld[h1 + fr + i] = fld[h1 + fr + i] * wrows[1, i]

    smooth(PASSES)

    def narrow(i, carry):
        for b in range(blocks):
            levels = slice(8 * b, 8 * b + 8)
            g = [fld[h1 + i, levels, p * mw : (p + 1) * mw] for p in range(4)]
            value = 0.625 * (g[0] + g[3]) + 0.875 * (g[1] + g[2])
            value = value + pltpu.roll(0.375 * g[0] + 0.125 * g[1], mw - 1, 1)
            blend[i, levels, :] = value + pltpu.roll(0.125 * g[2] + 0.375 * g[3], 1, 1)
        return carry

    lax.fori_loop(0, fr, narrow, 0)

    def gather(r, carry):
        weights = []
        place_of = (r + mr).astype(F32)
        for f in range(fr):
            source = jnp.broadcast_to(sf_ref[f, 0:1, :], (8, LANES)) - origin
            fraction = jnp.broadcast_to(sf_ref[f, 1:2, :], (8, LANES))
            lower = jnp.where(source == place_of, 1.0 - fraction, 0.0)
            weights.append(lower + jnp.where(source == place_of - 1.0, fraction, 0.0))
        for b in range(blocks):
            levels = slice(8 * b, 8 * b + 8)
            for t in range(qblocks):
                lanes = slice(t * LANES, (t + 1) * LANES)
                value = weights[0] * blend[0, levels, lanes]
                for f in range(1, fr):
                    value = value + weights[f] * blend[f, levels, lanes]
                contrib[r, levels, lanes] = value
        return carry

    lax.fori_loop(0, 3 * mr, gather, 0)
    a_up = lat_copy(12, 1, contrib.at[pl.ds(2 * mr, mr)], adjr.at[0])
    a_dn = lat_copy(13, -1, contrib.at[pl.ds(0, mr)], adjr.at[1])
    for item in (a_up, a_dn):
        start(item)
        pending.append(item)
    for at, absent in ((0, first), (1, last)):
        @pl.when(absent)
        def _():
            adjr[at] = zero_mid
    wait_recv(a_up)
    wait_recv(a_dn)
    fa[:, mine, :] = contrib[pl.ds(mr, mr)] + (adjr[0] + adjr[1])

    ag = []
    for k in range(1, nm):
        target = lax.rem(mem + k, nm)
        copy = pltpu.make_async_remote_copy(
            src_ref=fa.at[:, mine, :], dst_ref=fa.at[:, mine, :],
            send_sem=send_sem.at[16 + nm + k], recv_sem=recv_sem.at[16 + nm + k],
            device_id={"mem": target}, device_id_type=MESH,
        )
        copy.start()
        ag.append(copy)
    for k in range(1, nm):
        ag[k - 1].wait_recv()
    for copy in rs:
        copy.wait_send()
    for r in range(mr):
        for t in range(qblocks):
            ls[t, pl.ds(r, lv, stride=mr), :] = fa[r, :, t * LANES : (t + 1) * LANES]
    spread = jnp.concatenate([ls[t] for t in range(qblocks)], axis=1)

    down = down_ref[...]
    lont = lont_ref[...]
    for m in range(mb):
        parts = split3(pert[m].astype(F32) * spread)
        tall = dot(down, parts[0]) + (dot(down, parts[1]) + dot(down, parts[2]))
        thin = split3(tall)
        grad = dot(thin[0], lont) + (dot(thin[1], lont) + dot(thin[2], lont))
        for c in range(3):
            gp[c, m] = grad[c * cl : (c + 1) * cl]
    g_up = lat_copy(14, 1, gp.at[2], gpr.at[0])
    g_dn = lat_copy(15, -1, gp.at[0], gpr.at[1])
    for item in (g_up, g_dn):
        start(item)
        pending.append(item)

    @pl.when(first)
    def _():
        gpr[0] = gp[0]

    @pl.when(last)
    def _():
        gpr[1] = gp[2]

    wait_recv(g_up)
    wait_recv(g_dn)
    out_ref[...] = ctl_ref[...] + (gp[1] + (gpr[0] + gpr[1]))
    for item in pending:
        wait_send(item)
    for copy in ag:
        copy.wait_send()


def body(controls, perturbations, precision_weight, north_coef, east_coef, fine_source, fine_frac):
    nm, nl = lax.axis_size("mem"), lax.axis_size("lat")
    mb, cl, _, cw = controls.shape
    _, lv, mr, mw = perturbations.shape
    fr, fw = north_coef.shape
    lp = lv // nm
    h1, h2 = 2 * PASSES, PASSES
    ext = fr + 2 * h1
    level = refine_matrix(cl, "edge")
    across = refine_matrix(1, "pad")
    up = np.einsum("vc,ra->vrac", level, across).reshape(lv * mr, 3 * cl)
    lon = refine_matrix(cw, "wrap").T
    sf = jnp.stack([fine_source.astype(F32), fine_frac], axis=1)
    sf = jnp.broadcast_to(sf[:, :, None], (fr, 2, LANES))
    vmem = pl.BlockSpec(memory_space=pltpu.VMEM)
    anywhere = pl.BlockSpec(memory_space=pl.ANY)
    dims = (nm, nl, mb, cl, cw, lv, mr, mw, fr, fw)
    slots = 17 + 2 * nm
    result = pl.pallas_call(
        functools.partial(kernel, dims),
        out_shape=jax.ShapeDtypeStruct((mb, cl, cw), F32),
        in_specs=[vmem, anywhere, anywhere] + [vmem] * 7,
        out_specs=vmem,
        scratch_shapes=[
            pltpu.VMEM((2, mb, cl, cw), F32),
            pltpu.VMEM((mb, lv * mr, mw), BF16),
            pltpu.VMEM((lp, fr, fw), BF16),
            pltpu.VMEM((2, h2, lp, fw), F32),
            pltpu.VMEM((ext, 2, fw), F32),
            pltpu.VMEM((2 * h1, 2, LANES), F32),
            pltpu.VMEM((mw // LANES, lv * mr, LANES), F32),
            pltpu.VMEM((mr, lv, mw), F32),
            pltpu.VMEM((nm - 1, mr, lp, mw), F32),
            pltpu.VMEM((5 * mr, lp, mw), F32),
            pltpu.VMEM((ext, lp, fw), F32),
            pltpu.VMEM((fr, lp, mw), F32),
            pltpu.VMEM((3 * mr, lp, mw), F32),
            pltpu.VMEM((2, mr, lp, mw), F32),
            pltpu.VMEM((mr, lv, mw), F32),
            pltpu.VMEM((3, mb, cl, cw), F32),
            pltpu.VMEM((2, mb, cl, cw), F32),
            pltpu.VMEM((fr, lp, fw), F32),
            pltpu.SemaphoreType.DMA((2,)),
            pltpu.SemaphoreType.DMA((slots,)),
            pltpu.SemaphoreType.DMA((slots,)),
        ],
        compiler_params=pltpu.CompilerParams(collective_id=0, has_side_effects=True),
    )(
        controls.reshape(mb, cl, cw),
        perturbations.reshape(mb, lv * mr, mw),
        precision_weight,
        north_coef,
        east_coef,
        sf,
        jnp.asarray(np.concatenate([up] * 3, axis=1), BF16),
        jnp.asarray(lon, BF16),
        jnp.asarray(up.T, BF16),
        jnp.asarray(lon.T, BF16),
    )
    return result.reshape(controls.shape)


def solution(mesh):
    in_specs = (
        P("mem", None, "lat", None),
        P("mem", None, "lat", None),
        P(None, "lat", None),
        P("lat", None),
        P("lat", None),
        P("lat"),
        P("lat"),
    )
    out_specs = P("mem", None, "lat", None)
    return jax.shard_map(body, mesh=mesh, in_specs=in_specs, out_specs=out_specs, check_vma=False)
```

profile of v0, /device:TPU:1, one launch (start us, length us, event | category | flops | bytes accessed | tf_op | source)
XLA Modules:
  0.0 120.7 jit_solution(10149173406873631561)
XLA Ops:
  0.0 0.7 convert_bitcast_fusion
  0.7 0.7 pad_maximum_fusion
  1.3 0.1 copy.12
  1.4 0.7 broadcast_in_dim.2.sf_ref
  2.1 3.1 %reshape.11.pert_hbm = bf16[6,256,384]{2,1,0:T(8,128)(2,1)} reshape(bf16[6,64,4,384]{3,2,1,0:T(4,128)(2,1)} %param.12) | data formatting | bytes 2359296 | tf_op jit(solution)/shard_map/reshape | solution.py:488
  5.2 114.1 %shard_map.109 = f32[6,16,96]{2,1,0:T(8,128)} custom-call(f32[6,16,96]{2,1,0:T(8,128)} %bitcast.8, bf16[6,256,384]{2,1,0:T(8,128)(2,1)} %reshape.11.pert_hbm, bf16[64,16,1536]{2,1,0:T(8,128)(2,1)} %pw_hbm.1, f32[16,1536]{1,0:T(8,128)} %north_ref.1, f32[16,1536]{1,0:T(8,128)} %east_ref.1, f32[16,2,128]{2,1,0:T(2,128)} %broadcast_in_dim.2.sf_ref, ...), custom_call_target="tpu_custom_call" | custom-call | tf_op jit(solution)/shard_map/pallas_call | solution.py:457
  119.3 1.4 %copy.15 = f32[6,16,1,96]{3,2,1,0:T(1,128)} copy(f32[6,16,1,96]{3,2,1,0:T(1,128)} %bitcast.7) | data formatting | bytes 73728
where the time goes:
time: 121 us
  Pallas kernels  114 us (94%)
  local copies, waits for them, and re-layouts  5.34 us (4%)
  other arithmetic  1.32 us (1%)
    pallas_call x1, Pallas kernels, body(): pl.pallas_call(functools.partial(kernel, dims), out_shape=jax.ShapeDtypeS...  114 us
    reshape x1, local copies, waits for them, and re-layouts, body(): perturbations.reshape(mb, lv * mr, mw)  3.15 us

commit v1 on v0

--- a/solution.py
+++ b/solution.py
@@ -10,6 +10,7 @@
 PASSES = 5
 REACH = 4
 LANES = 128
+UNROLL = 8
 F32 = jnp.float32
 BF16 = jnp.bfloat16
 MESH = pl.DeviceIdType.MESH
@@ -132,15 +133,21 @@
 
     for kind, ref in enumerate((north_ref, east_ref)):
         stacked = jnp.concatenate(split3(ref[...]), axis=0)
+        edges = []
         for block in range(qblocks):
             moved = dot(stacked[:, block * 4 * LANES : (block + 1) * 4 * LANES], perm)
             exact = (moved[:fr] + moved[fr : 2 * fr]) + moved[2 * fr :]
+            edges.append(exact[:, 3 * LANES :])
             for phase in range(4):
                 lanes = pl.ds(phase * mw + block * LANES, LANES)
                 for row in range(fr):
                     co[h1 + row, kind : kind + 1, lanes] = exact[
                         row : row + 1, phase * LANES : (phase + 1) * LANES
                     ]
+    edge = pltpu.roll(jnp.concatenate(edges, axis=1), 1, 1)
+    for row in range(fr):
+        co[h1 + row, 2:3, 0:mw] = edge[row : row + 1]
+        co[h1 + row, 2:3, mw:fw] = jnp.zeros((1, fw - mw), F32)
     k_up = lat_copy(4, 1, co.at[pl.ds(fr, h1)], co.at[pl.ds(0, h1)])
     k_dn = lat_copy(5, -1, co.at[pl.ds(h1, h1)], co.at[pl.ds(h1 + fr, h1)])
     for item in (k_up, k_dn):
@@ -228,12 +235,15 @@
 
     @pl.when(first)
     def _():
-        fld[h1 - 1] = jnp.zeros((lp, fw), F32)
-        co[h1 - 1] = jnp.zeros((2, fw), F32)
+        for row in range(h1):
+            fld[row] = jnp.zeros((lp, fw), F32)
+            co[row] = jnp.zeros((3, fw), F32)
 
     @pl.when(last)
     def _():
-        fld[h1 + fr] = jnp.zeros((lp, fw), F32)
+        for row in range(h1):
+            fld[h1 + fr + row] = jnp.zeros((lp, fw), F32)
+            co[h1 + fr + row] = jnp.zeros((3, fw), F32)
 
     for item in (s_up, s_dn, *near, k_up, k_dn):
         wait_recv(item)
@@ -282,7 +292,7 @@
     def _():
         make_rows(sfr, h1, h1 + fr, h1, 2 * mr)
 
-    def one_pass(low, high):
+    def one_pass(low, steps):
         for b in range(blocks):
             levels = slice(8 * b, 8 * b + 8)
 
@@ -296,26 +306,34 @@
             under = phases(low - 1)
             flux0 = [coef(low - 1, 0, p) * (centre0[p] - under[p]) for p in range(4)]
 
-            def step(row, carry):
+            def step(i, carry):
                 now, below_flux = carry
-                over = phases(row + 1)
-                east = [coef(row, 1, p) * (now[p + 1] - now[p]) for p in range(3)]
-                east.append(coef(row, 1, 3) * (pltpu.roll(now[0], mw - 1, 1) - now[3]))
-                west = [pltpu.roll(east[3], 1, 1)] + east[:3]
-                north = [coef(row, 0, p) * (over[p] - now[p]) for p in range(4)]
-                for p in range(4):
-                    fld[row, levels, p * mw : (p + 1) * mw] = now[p] + (
-                        (north[p] - below_flux[p]) + (east[p] - west[p])
-                    )
-                return over, north
-
-            lax.fori_loop(low, high, step, (centre0, flux0))
+                for u in range(UNROLL):
+                    row = low + i * UNROLL + u
+                    over = phases(row + 1)
+                    east = [coef(row, 1, p) * (now[p + 1] - now[p]) for p in range(3)]
+                    east.append(coef(row, 1, 3) * (pltpu.roll(now[0], mw - 1, 1) - now[3]))
+                    edge = coef(row, 2, 0) * (now[0] - pltpu.roll(now[3], 1, 1))
+                    west = [edge] + east[:3]
+                    north = [coef(row, 0, p) * (over[p] - now[p]) for p in range(4)]
+                    for p in range(4):
+                        fld[row, levels, p * mw : (p + 1) * mw] = now[p] + (
+                            (north[p] - below_flux[p]) + (east[p] - west[p])
+                        )
+                    now, below_flux = over, north
+                return now, below_flux
+
+            lax.fori_loop(0, steps, step, (centre0, flux0))
 
     def smooth(margin):
         def body(p, carry):
-            low = jnp.where(first, h1, margin + 1 + p)
-            high = jnp.where(last, h1 + fr, ext - margin - 1 - p)
-            one_pass(low, high)
+            low = margin + 1 + p
+            one_pass(low, lax.div(ext - 2 * low + UNROLL - 1, UNROLL))
+
+            @pl.when(last)
+            def _():
+                fld[h1 + fr] = jnp.zeros((lp, fw), F32)
+
             return carry
 
         lax.fori_loop(0, PASSES, body, 0)
@@ -464,13 +482,13 @@
             pltpu.VMEM((mb, lv * mr, mw), BF16),
             pltpu.VMEM((lp, fr, fw), BF16),
             pltpu.VMEM((2, h2, lp, fw), F32),
-            pltpu.VMEM((ext, 2, fw), F32),
+            pltpu.VMEM((ext + UNROLL, 3, fw), F32),
             pltpu.VMEM((2 * h1, 2, LANES), F32),
             pltpu.VMEM((mw // LANES, lv * mr, LANES), F32),
             pltpu.VMEM((mr, lv, mw), F32),
             pltpu.VMEM((nm - 1, mr, lp, mw), F32),
             pltpu.VMEM((5 * mr, lp, mw), F32),
-            pltpu.VMEM((ext, lp, fw), F32),
+            pltpu.VMEM((ext + UNROLL, lp, fw), F32),
             pltpu.VMEM((fr, lp, mw), F32),
             pltpu.VMEM((3 * mr, lp, mw), F32),
             pltpu.VMEM((2, mr, lp, mw), F32),

time: 121 us -> 58.9 us (0.49)
  Pallas kernels: 114 us -> 52 us
    pallas_call x1, Pallas kernels: 114 us -> 52 us  [body(): pl.pallas_call(functools.partial(kernel, dims), out_shape=jax.ShapeDtypeS...]
where the time goes in v1:
time: 58.9 us; the launch traced here: 58.7 us
  Pallas kernels  52 us (88%)
  local copies, waits for them, and re-layouts  5.34 us (9%)
  other arithmetic  1.32 us (2%)
    pallas_call x1, Pallas kernels, body(): pl.pallas_call(functools.partial(kernel, dims), out_shape=jax.ShapeDtypeS...  52 us
    reshape x1, local copies, waits for them, and re-layouts, body(): perturbations.reshape(mb, lv * mr, mw)  3.15 us
    unnamed x1, local copies, waits for them, and re-layouts  1.42 us
    another operation x2, other arithmetic, body(): sf = jnp.stack([fine_source.astype(F32), fine_frac], axis=1)  1.32 us

profile of v1, /device:TPU:1, one launch (start us, length us, event | category | flops | bytes accessed | tf_op | source)
XLA Modules:
  0.0 58.7 jit_solution(10354801980449872687)
XLA Ops:
  0.0 0.7 %convert_bitcast_fusion = f32[16,1]{0,1:T(1,128)S(1)} fusion(s32[16]{0:T(128)} %param.16), kind=kLoop, calls=%fused_computation.1 | loop fusion | flops 16 | bytes 128 | tf_op jit(solution)/shard_map/stack | solution.py:469
  0.7 0.7 %pad_maximum_fusion = f32[16,2]{0,1:T(2,128)S(1)} fusion(f32[16,1]{0,1:T(1,128)} %bitcast.9, f32[16,1]{0,1:T(1,128)S(1)} %convert_bitcast_fusion), kind=kLoop, calls=%fused_computation | loop fusion | flops 32 | bytes 256 | tf_op jit(solution)/shard_map/stack | solution.py:469
  1.3 0.1 copy.12
  1.4 0.7 %broadcast_in_dim.2.sf_ref = f32[16,2,128]{2,1,0:T(2,128)} broadcast(f32[16,2]{1,0:T(8,128)S(1)} %copy.12), dimensions={0,1} | broadcast | bytes 16512 | tf_op jit(solution)/shard_map/broadcast_in_dim | solution.py:470
  2.1 3.1 %reshape.11.pert_hbm = bf16[6,256,384]{2,1,0:T(8,128)(2,1)} reshape(bf16[6,64,4,384]{3,2,1,0:T(4,128)(2,1)} %param.12) | data formatting | bytes 2359296 | tf_op jit(solution)/shard_map/reshape | solution.py:506
  5.2 52.0 %shard_map.109 = f32[6,16,96]{2,1,0:T(8,128)} custom-call(f32[6,16,96]{2,1,0:T(8,128)} %bitcast.8, bf16[6,256,384]{2,1,0:T(8,128)(2,1)} %reshape.11.pert_hbm, bf16[64,16,1536]{2,1,0:T(8,128)(2,1)} %pw_hbm.1, f32[16,1536]{1,0:T(8,128)} %north_ref.1, f32[16,1536]{1,0:T(8,128)} %east_ref.1, f32[16,2,128]{2,1,0:T(2,128)} %broadcast_in_dim.2.sf_ref, ...), custom_call_target="tpu_custom_call" | custom-call | tf_op jit(solution)/shard_map/pallas_call | solution.py:475
  57.2 1.4 %copy.15 = f32[6,16,1,96]{3,2,1,0:T(1,128)} copy(f32[6,16,1,96]{3,2,1,0:T(1,128)} %bitcast.7) | data formatting | bytes 73728

commit v2 on v0

v2 whole, which is shorter than its diff:
```python
import functools
import jax
import jax.numpy as jnp
import numpy as np
from jax import lax
from jax.experimental import pallas as pl
from jax.experimental.pallas import tpu as pltpu
from jax.sharding import PartitionSpec as P

PASSES = 5
REACH = 4
LANES = 128
UNROLL = 8
F32 = jnp.float32
BF16 = jnp.bfloat16
MESH = pl.DeviceIdType.MESH


def refine_matrix(count, mode):
    weights = [(0.375, 0.625, 0.0), (0.125, 0.875, 0.0), (0.0, 0.875, 0.125), (0.0, 0.625, 0.375)]
    full = np.zeros((4 * count, count + 2), np.float32)
    for q in range(count):
        for r in range(4):
            full[4 * q + r, q : q + 3] += weights[r]
    if mode == "pad":
        return full
    inner = full[:, 1:-1].copy()
    if mode == "edge":
        inner[:, 0] += full[:, 0]
        inner[:, -1] += full[:, -1]
    else:
        inner[:, -1] += full[:, 0]
        inner[:, 0] += full[:, -1]
    return inner


def split3(value):
    high = value.astype(BF16)
    rest = value - high.astype(F32)
    mid = rest.astype(BF16)
    low = (rest - mid.astype(F32)).astype(BF16)
    return high, mid, low


def dot(a, b):
    return jnp.dot(a, b, preferred_element_type=F32)


def kernel(
    dims,
    ctl_ref, pert_hbm, pw_hbm, north_ref, east_ref, source_ref, frac_ref, up_ref, lon_ref, down_ref, lont_ref,
    out_ref,
    ctl, pert, pw, wrows, co, wt, ls, mids, rsr, midx, fld, blend, contrib, adjr, fa, gp, gpr, wown,
    local_sem, send_sem, recv_sem,
):
    nm, nl, mb, cl, cw, lv, mr, mw, fr, fw = dims
    lp = lv // nm
    h1, h2 = 2 * PASSES, PASSES
    ext = fr + 2 * h1
    mem, lat = lax.axis_index("mem"), lax.axis_index("lat")
    first, last = lat == 0, lat == nl - 1
    blocks = lp // 8
    taps = wt.shape[1]

    cp_pert = pltpu.make_async_copy(pert_hbm, pert, local_sem.at[0])
    cp_pert.start()
    cp_pw = pltpu.make_async_copy(
        pw_hbm.at[pl.ds(mem * lp, lp)], pw, local_sem.at[1]
    )
    cp_pw.start()

    barrier = pltpu.get_barrier_semaphore()
    for step in (1, 2):
        @pl.when(lat >= step)
        def _():
            pl.semaphore_signal(barrier, inc=1, device_id={"lat": lat - step}, device_id_type=MESH)

        @pl.when(lat < nl - step)
        def _():
            pl.semaphore_signal(barrier, inc=1, device_id={"lat": lat + step}, device_id_type=MESH)
    for k in range(1, nm):
        pl.semaphore_signal(
            barrier, inc=1, device_id={"mem": lax.rem(mem + k, nm)}, device_id_type=MESH
        )
    present = nm - 1
    for step in (1, 2):
        present = present + (lat >= step).astype(jnp.int32) + (lat < nl - step).astype(jnp.int32)

    spot = lax.broadcasted_iota(jnp.int32, (taps, LANES), 0)
    for row in range(fr):
        place = source_ref[row] - (lat * mr - mr)
        upper = jnp.full((taps, LANES), frac_ref[row], F32)
        wt[h1 + row] = jnp.where(
            spot == place, 1.0 - upper, jnp.where(spot == place + 1, upper, 0.0)
        )

    rows_i = lax.broadcasted_iota(jnp.int32, (4 * LANES, 4 * LANES), 0)
    cols_i = lax.broadcasted_iota(jnp.int32, (4 * LANES, 4 * LANES), 1)
    perm = (rows_i == 4 * lax.rem(cols_i, LANES) + lax.div(cols_i, LANES)).astype(F32).astype(BF16)
    qblocks = mw // LANES

    for kind, ref in enumerate((north_ref, east_ref)):
        stacked = jnp.concatenate(split3(ref[...]), axis=0)
        edges = []
        for block in range(qblocks):
            moved = dot(stacked[:, block * 4 * LANES : (block + 1) * 4 * LANES], perm)
            exact = (moved[:fr] + moved[fr : 2 * fr]) + moved[2 * fr :]
            edges.append(exact[:, 3 * LANES :])
            for phase in range(4):
                lanes = pl.ds(phase * mw + block * LANES, LANES)
                for row in range(fr):
                    co[h1 + row, kind : kind + 1, lanes] = exact[
                        row : row + 1, phase * LANES : (phase + 1) * LANES
                    ]
    edge = pltpu.roll(jnp.concatenate(edges, axis=1), 1, 1)
    for row in range(fr):
        co[h1 + row, 2:3, 0:mw] = edge[row : row + 1]
        co[h1 + row, 2:3, mw:fw] = jnp.zeros((1, fw - mw), F32)
    pl.semaphore_wait(barrier, present)

    def lat_copy(slot, step, src, dst):
        copy = pltpu.make_async_remote_copy(
            src_ref=src, dst_ref=dst, send_sem=send_sem.at[slot], recv_sem=recv_sem.at[slot],
            device_id={"lat": lat + step}, device_id_type=MESH,
        )
        if step > 0:
            return copy, lat < nl - step, lat >= step
        return copy, lat >= -step, lat < nl + step

    def start(item):
        copy, sends, _ = item

        @pl.when(sends)
        def _():
            copy.start()

    def wait_recv(item):
        copy, _, receives = item

        @pl.when(receives)
        def _():
            copy.wait_recv()

    def wait_send(item):
        copy, sends, _ = item

        @pl.when(sends)
        def _():
            copy.wait_send()

    pending = []

    c_up = lat_copy(0, 1, ctl_ref, ctl.at[0])
    c_dn = lat_copy(1, -1, ctl_ref, ctl.at[1])
    k_up = lat_copy(4, 1, co.at[pl.ds(fr, h1)], co.at[pl.ds(0, h1)])
    k_dn = lat_copy(5, -1, co.at[pl.ds(h1, h1)], co.at[pl.ds(h1 + fr, h1)])
    s_up = lat_copy(2, 1, wt.at[pl.ds(fr, h1)], wt.at[pl.ds(0, h1)])
    s_dn = lat_copy(3, -1, wt.at[pl.ds(h1, h1)], wt.at[pl.ds(h1 + fr, h1)])
    for item in (c_up, c_dn, s_up, s_dn, k_up, k_dn):
        start(item)
        pending.append(item)

    cp_pw.wait()
    count = lp * fr
    to_i = lax.broadcasted_iota(jnp.int32, (count, count), 0)
    from_i = lax.broadcasted_iota(jnp.int32, (count, count), 1)
    turn = (from_i == lax.rem(to_i, lp) * fr + lax.div(to_i, lp)).astype(F32).astype(BF16)
    for block in range(qblocks):
        piece = pw[:, :, block * 4 * LANES : (block + 1) * 4 * LANES].reshape(count, 4 * LANES)
        turned = dot(turn, piece).astype(BF16)
        moved = dot(turned, perm)
        for phase in range(4):
            lanes = pl.ds(phase * mw + block * LANES, LANES)
            wown[:, :, lanes] = moved[:, phase * LANES : (phase + 1) * LANES].reshape(fr, lp, LANES)
    w_up = lat_copy(6, 1, wown.at[pl.ds(fr - h2, h2)], wrows.at[0])
    w_dn = lat_copy(7, -1, wown.at[pl.ds(0, h2)], wrows.at[1])
    for item in (w_up, w_dn):
        start(item)
        pending.append(item)

    wait_recv(c_up)
    wait_recv(c_dn)
    own = ctl_ref[...]
    below = jnp.where(first, own, ctl[0])
    above = jnp.where(last, own, ctl[1])
    lon = lon_ref[...]
    wide = []
    for part in (below, own, above):
        parts = split3(part.reshape(mb * cl, cw))
        wide.append(dot(parts[0], lon) + (dot(parts[1], lon) + dot(parts[2], lon)))
    cp_pert.wait()
    up3 = up_ref[...]
    for m in range(mb):
        stack = jnp.concatenate([w[m * cl : (m + 1) * cl] for w in wide], axis=0)
        raised = dot(up3, jnp.concatenate(split3(stack), axis=0))
        term = pert[m].astype(F32).reshape(lv * mr, mw) * raised
        for t in range(qblocks):
            piece = term[:, t * LANES : (t + 1) * LANES]
            if m == 0:
                ls[t] = piece
            else:
                ls[t] += piece
    for r in range(mr):
        for t in range(qblocks):
            mids[r, :, t * LANES : (t + 1) * LANES] = ls[t, pl.ds(r, lv, stride=mr), :]

    def block_levels(b):
        return pl.ds(8 * b, 8)

    def mem_slice(device, b):
        return pl.ds(pl.multiple_of(device * lp + 8 * b, 8), 8)

    rs = {}
    for b in range(blocks):
        for k in range(1, nm):
            target = lax.rem(mem + k, nm)
            slot = 10 + 6 * blocks + (b * nm + k)
            copy = pltpu.make_async_remote_copy(
                src_ref=mids.at[:, mem_slice(target, b), :],
                dst_ref=rsr.at[k - 1, :, block_levels(b), :],
                send_sem=send_sem.at[slot], recv_sem=recv_sem.at[slot],
                device_id={"mem": target}, device_id_type=MESH,
            )
            copy.start()
            rs[b, k] = copy

    centre = 2 * mr
    zero_mid = jnp.zeros((mr, lp, mw), F32)
    for at, absent in ((1, first), (0, lat < 2), (3, last), (4, lat >= nl - 2)):
        @pl.when(absent)
        def _():
            midx[pl.ds(at * mr, mr)] = zero_mid

    @pl.when(first)
    def _():
        adjr[0] = zero_mid
        for row in range(h1):
            fld[row] = jnp.zeros((lp, fw), F32)
            co[row] = jnp.zeros((3, fw), F32)

    @pl.when(last)
    def _():
        adjr[1] = zero_mid
        for row in range(h1):
            fld[h1 + fr + row] = jnp.zeros((lp, fw), F32)
            co[h1 + fr + row] = jnp.zeros((3, fw), F32)

    def add_up(b):
        levels = slice(8 * b, 8 * b + 8)
        total = mids[:, mem_slice(mem, b), :]
        for k in range(1, nm):
            rs[b, k].wait_recv()
            total = total + rsr[k - 1, :, levels, :]
        midx[pl.ds(centre, mr), levels, :] = total
        items = []
        for place, step in enumerate((1, -1, 2, -2)):
            item = lat_copy(
                10 + 4 * b + place, step,
                midx.at[pl.ds(centre, mr), block_levels(b), :],
                midx.at[pl.ds(centre - step * mr, mr), block_levels(b), :],
            )
            start(item)
            pending.append(item)
            items.append(item)
        return items

    def make_rows(b, at, rows, base, unroll):
        levels = slice(8 * b, 8 * b + 8)

        def one(i):
            row = []
            shares = [
                jnp.broadcast_to(wt[i, r : r + 1, :], (8, LANES)) for r in range(3 * mr)
            ]
            for t in range(qblocks):
                lanes = slice(t * LANES, (t + 1) * LANES)
                value = shares[0] * midx[base, levels, lanes]
                for r in range(1, 3 * mr):
                    value = value + shares[r] * midx[base + r, levels, lanes]
                row.append(value)
            row = jnp.concatenate(row, axis=1)
            before = pltpu.roll(row, 1, 1)
            after = pltpu.roll(row, mw - 1, 1)
            fld[i, levels, 0:mw] = 0.375 * before + 0.625 * row
            fld[i, levels, mw : 2 * mw] = 0.125 * before + 0.875 * row
            fld[i, levels, 2 * mw : 3 * mw] = 0.875 * row + 0.125 * after
            fld[i, levels, 3 * mw : 4 * mw] = 0.625 * row + 0.375 * after

        def step(i, carry):
            for u in range(unroll):
                one(at + i * unroll + u)
            return carry

        lax.fori_loop(0, rows // unroll, step, 0)

    def one_pass(b, low, steps):
        levels = slice(8 * b, 8 * b + 8)

        def phases(row):
            return [fld[row, levels, p * mw : (p + 1) * mw] for p in range(4)]

        def coef(row, kind, p):
            return co[row, kind : kind + 1, p * mw : (p + 1) * mw]

        centre0 = phases(low)
        under = phases(low - 1)
        flux0 = [coef(low - 1, 0, p) * (centre0[p] - under[p]) for p in range(4)]

        def step(i, carry):
            now, below_flux = carry
            for u in range(UNROLL):
                row = low + i * UNROLL + u
                over = phases(row + 1)
                east = [coef(row, 1, p) * (now[p + 1] - now[p]) for p in range(3)]
                east.append(coef(row, 1, 3) * (pltpu.roll(now[0], mw - 1, 1) - now[3]))
                edge = coef(row, 2, 0) * (now[0] - pltpu.roll(now[3], 1, 1))
                west = [edge] + east[:3]
                north = [coef(row, 0, p) * (over[p] - now[p]) for p in range(4)]
                for p in range(4):
                    fld[row, levels, p * mw : (p + 1) * mw] = now[p] + (
                        (north[p] - below_flux[p]) + (east[p] - west[p])
                    )
                now, below_flux = over, north
            return now, below_flux

        lax.fori_loop(0, steps, step, (centre0, flux0))

    def smooth(b, margin):
        levels = slice(8 * b, 8 * b + 8)

        def body(p, carry):
            low = margin + 1 + p
            one_pass(b, low, lax.div(ext - 2 * low + UNROLL - 1, UNROLL))

            @pl.when(last)
            def _():
                fld[h1 + fr, levels, :] = jnp.zeros((8, fw), F32)

            return carry

        lax.fori_loop(0, PASSES, body, 0)

    def apply_weights(b):
        levels = slice(8 * b, 8 * b + 8)

        def apply_own(i, carry):
            for u in range(4):
                row = 4 * i + u
                fld[h1 + row, levels, :] = fld[h1 + row, levels, :] * wown[row, levels, :]
            return carry

        lax.fori_loop(0, fr // 4, apply_own, 0)

        @pl.when(jnp.logical_not(first))
        def _():
            for i in range(h2):
                at = h1 - h2 + i
                fld[at, levels, :] = fld[at, levels, :] * wrows[0, i, levels, :]

        @pl.when(jnp.logical_not(last))
        def _():
            for i in range(h2):
                at = h1 + fr + i
                fld[at, levels, :] = fld[at, levels, :] * wrows[1, i, levels, :]

    def transpose_rows(b):
        levels = slice(8 * b, 8 * b + 8)

        def narrow(step, carry):
            for u in range(4):
                i = 4 * step + u
                g = [fld[h1 + i, levels, p * mw : (p + 1) * mw] for p in range(4)]
                value = 0.625 * (g[0] + g[3]) + 0.875 * (g[1] + g[2])
                value = value + pltpu.roll(0.375 * g[0] + 0.125 * g[1], mw - 1, 1)
                blend[i, levels, :] = value + pltpu.roll(0.125 * g[2] + 0.375 * g[3], 1, 1)
            return carry

        lax.fori_loop(0, fr // 4, narrow, 0)

        def gather(r):
            shares = [
                jnp.broadcast_to(wt[h1 + f, r : r + 1, :], (8, LANES)) for f in range(fr)
            ]
            for t in range(qblocks):
                lanes = slice(t * LANES, (t + 1) * LANES)
                value = shares[0] * blend[0, levels, lanes]
                for f in range(1, fr):
                    value = value + shares[f] * blend[f, levels, lanes]
                contrib[r, levels, lanes] = value

        for r in list(range(mr)) + list(range(2 * mr, 3 * mr)):
            gather(r)
        items = []
        for place, step, at in ((0, 1, 2 * mr), (1, -1, 0)):
            item = lat_copy(
                10 + 4 * blocks + 2 * b + place, step,
                contrib.at[pl.ds(at, mr), block_levels(b), :],
                adjr.at[place, :, block_levels(b), :],
            )
            start(item)
            pending.append(item)
            items.append(item)
        for r in range(mr, 2 * mr):
            gather(r)
        return items

    ag = {}

    def share(b, items):
        levels = slice(8 * b, 8 * b + 8)
        for item in items:
            wait_recv(item)
        mine = mem_slice(mem, b)
        fa[:, mine, :] = contrib[pl.ds(mr, mr), levels, :] + (
            adjr[0, :, levels, :] + adjr[1, :, levels, :]
        )
        for k in range(1, nm):
            target = lax.rem(mem + k, nm)
            slot = 10 + 6 * blocks + ((blocks + b) * nm + k)
            copy = pltpu.make_async_remote_copy(
                src_ref=fa.at[:, mine, :], dst_ref=fa.at[:, mine, :],
                send_sem=send_sem.at[slot], recv_sem=recv_sem.at[slot],
                device_id={"mem": target}, device_id_type=MESH,
            )
            copy.start()
            ag[b, k] = copy

    near = {0: add_up(0)}
    previous = None
    for b in range(blocks):
        if b == 0:
            wait_recv(s_up)
            wait_recv(s_dn)
        for item in near[b][:2]:
            wait_recv(item)
        make_rows(b, h1, fr, mr, 4)
        for item in near[b][2:]:
            wait_recv(item)

        @pl.when(jnp.logical_not(first))
        def _():
            make_rows(b, 0, h1, 0, 5)

        @pl.when(jnp.logical_not(last))
        def _():
            make_rows(b, h1 + fr, h1, 2 * mr, 5)

        if b + 1 < blocks:
            near[b + 1] = add_up(b + 1)
        if b == 0:
            wait_recv(k_up)
            wait_recv(k_dn)
        smooth(b, 0)
        if previous is not None:
            share(b - 1, previous)
        if b == 0:
            wait_recv(w_up)
            wait_recv(w_dn)
        apply_weights(b)
        smooth(b, PASSES)
        previous = transpose_rows(b)
    share(blocks - 1, previous)
    for copy in ag.values():
        copy.wait_recv()
    for copy in rs.values():
        copy.wait_send()
    for r in range(mr):
        for t in range(qblocks):
            ls[t, pl.ds(r, lv, stride=mr), :] = fa[r, :, t * LANES : (t + 1) * LANES]
    spread = jnp.concatenate([ls[t] for t in range(qblocks)], axis=1)

    down = down_ref[...]
    lont = lont_ref[...]
    for m in range(mb):
        parts = split3(pert[m].astype(F32).reshape(lv * mr, mw) * spread)
        tall = dot(down, parts[0]) + (dot(down, parts[1]) + dot(down, parts[2]))
        thin = split3(tall)
        grad = dot(thin[0], lont) + (dot(thin[1], lont) + dot(thin[2], lont))
        for c in range(3):
            gp[c, m] = grad[c * cl : (c + 1) * cl]
    g_up = lat_copy(8, 1, gp.at[2], gpr.at[0])
    g_dn = lat_copy(9, -1, gp.at[0], gpr.at[1])
    for item in (g_up, g_dn):
        start(item)
        pending.append(item)

    @pl.when(first)
    def _():
        gpr[0] = gp[0]

    @pl.when(last)
    def _():
        gpr[1] = gp[2]

    wait_recv(g_up)
    wait_recv(g_dn)
    out_ref[...] = ctl_ref[...] + (gp[1] + (gpr[0] + gpr[1]))
    for item in pending:
        wait_send(item)
    for copy in ag.values():
        copy.wait_send()


def body(controls, perturbations, precision_weight, north_coef, east_coef, fine_source, fine_frac):
    nm, nl = lax.axis_size("mem"), lax.axis_size("lat")
    mb, cl, _, cw = controls.shape
    _, lv, mr, mw = perturbations.shape
    fr, fw = north_coef.shape
    lp = lv // nm
    h1, h2 = 2 * PASSES, PASSES
    ext = fr + 2 * h1
    level = refine_matrix(cl, "edge")
    across = refine_matrix(1, "pad")
    up = np.einsum("vc,ra->vrac", level, across).reshape(lv * mr, 3 * cl)
    lon = refine_matrix(cw, "wrap").T
    vmem = pl.BlockSpec(memory_space=pltpu.VMEM)
    smem = pl.BlockSpec(memory_space=pltpu.SMEM)
    anywhere = pl.BlockSpec(memory_space=pl.ANY)
    dims = (nm, nl, mb, cl, cw, lv, mr, mw, fr, fw)
    blocks = lp // 8
    slots = 10 + 6 * blocks + 2 * blocks * nm
    taps = -(-3 * mr // 8) * 8
    result = pl.pallas_call(
        functools.partial(kernel, dims),
        out_shape=jax.ShapeDtypeStruct((mb, cl, cw), F32),
        in_specs=[vmem, anywhere, anywhere, vmem, vmem, smem, smem] + [vmem] * 4,
        out_specs=vmem,
        scratch_shapes=[
            pltpu.VMEM((2, mb, cl, cw), F32),
            pltpu.VMEM((mb, lv, mr, mw), BF16),
            pltpu.VMEM((lp, fr, fw), BF16),
            pltpu.VMEM((2, h2, lp, fw), F32),
            pltpu.VMEM((ext + UNROLL, 3, fw), F32),
            pltpu.VMEM((ext, taps, LANES), F32),
            pltpu.VMEM((mw // LANES, lv * mr, LANES), F32),
            pltpu.VMEM((mr, lv, mw), F32),
            pltpu.VMEM((nm - 1, mr, lp, mw), F32),
            pltpu.VMEM((5 * mr, lp, mw), F32),
            pltpu.VMEM((ext + UNROLL, lp, fw), F32),
            pltpu.VMEM((fr, lp, mw), F32),
            pltpu.VMEM((3 * mr, lp, mw), F32),
            pltpu.VMEM((2, mr, lp, mw), F32),
            pltpu.VMEM((mr, lv, mw), F32),
            pltpu.VMEM((3, mb, cl, cw), F32),
            pltpu.VMEM((2, mb, cl, cw), F32),
            pltpu.VMEM((fr, lp, fw), F32),
            pltpu.SemaphoreType.DMA((2,)),
            pltpu.SemaphoreType.DMA((slots,)),
            pltpu.SemaphoreType.DMA((slots,)),
        ],
        compiler_params=pltpu.CompilerParams(collective_id=0, has_side_effects=True),
    )(
        controls.reshape(mb, cl, cw),
        perturbations,
        precision_weight,
        north_coef,
        east_coef,
        fine_source,
        fine_frac,
        jnp.asarray(np.concatenate([up] * 3, axis=1), BF16),
        jnp.asarray(lon, BF16),
        jnp.asarray(up.T, BF16),
        jnp.asarray(lon.T, BF16),
    )
    return result.reshape(controls.shape)


def solution(mesh):
    in_specs = (
        P("mem", None, "lat", None),
        P("mem", None, "lat", None),
        P(None, "lat", None),
        P("lat", None),
        P("lat", None),
        P("lat"),
        P("lat"),
    )
    out_specs = P("mem", None, "lat", None)
    return jax.shard_map(body, mesh=mesh, in_specs=in_specs, out_specs=out_specs, check_vma=False)
```

time: 121 us -> 46 us (0.38)
  Pallas kernels: 114 us -> 44.4 us
  local copies, waits for them, and re-layouts: 5.34 us -> 1.42 us
  other arithmetic: 1.32 us -> 0 us
    pallas_call x1, Pallas kernels: 114 us -> 44.4 us  [body(): pl.pallas_call(functools.partial(kernel, dims), out_shape=jax.ShapeDtypeS...]
    reshape x1 -> x0, local copies, waits for them, and re-layouts: 3.15 us -> none  [body(): perturbations.reshape(mb, lv * mr, mw)]
    another operation x2 -> x0, other arithmetic: 1.32 us -> none  [body(): sf = jnp.stack([fine_source.astype(F32), fine_frac], axis=1)]
where the time goes in v2:
time: 46 us; the launch traced here: 45.8 us
  Pallas kernels  44.4 us (97%)
  local copies, waits for them, and re-layouts  1.42 us (3%)
    pallas_call x1, Pallas kernels, body(): pl.pallas_call(functools.partial(kernel, dims), out_shape=jax.ShapeDtypeS...  44.4 us
    unnamed x1, local copies, waits for them, and re-layouts  1.42 us

profile of v2, /device:TPU:1, one launch (start us, length us, event | category | flops | bytes accessed | tf_op | source)
XLA Modules:
  0.0 45.8 jit_solution(16303121340966883492)
XLA Ops:
  0.0 44.4 %shard_map.109 = f32[6,16,96]{2,1,0:T(8,128)} custom-call(f32[6,16,96]{2,1,0:T(8,128)} %bitcast.5, bf16[6,64,4,384]{3,2,1,0:T(4,128)(2,1)} %pert_hbm.1, bf16[64,16,1536]{2,1,0:T(8,128)(2,1)} %pw_hbm.1, f32[16,1536]{1,0:T(8,128)} %north_ref.1, f32[16,1536]{1,0:T(8,128)} %east_ref.1, s32[16]{0:T(128)} %source_ref.1, f32[16]{0:T(128)} %frac_ref.1, ...), custom_call_target="tpu_custom_call" | custom-call | tf_op jit(solution)/shard_map/pallas_call | solution.py:523
  44.4 1.4 %copy.14 = f32[6,16,1,96]{3,2,1,0:T(1,128)} copy(f32[6,16,1,96]{3,2,1,0:T(1,128)} %bitcast.4) | data formatting | bytes 73728

commit v3 on v2

--- a/solution.py
+++ b/solution.py
@@ -42,6 +42,11 @@
     return high, mid, low
 
 
+def split2(value):
+    high = value.astype(BF16)
+    return high, (value - high.astype(F32)).astype(BF16)
+
+
 def dot(a, b):
     return jnp.dot(a, b, preferred_element_type=F32)
 
@@ -50,7 +55,7 @@
     dims,
     ctl_ref, pert_hbm, pw_hbm, north_ref, east_ref, source_ref, frac_ref, up_ref, lon_ref, down_ref, lont_ref,
     out_ref,
-    ctl, pert, pw, wrows, co, wt, ls, mids, rsr, midx, fld, blend, contrib, adjr, fa, gp, gpr, wown,
+    ctl, pert, pw, wrows, co, wt, ls, mids, rsr, midx, fld, blend, contrib, adjr, fa, gp, gpr, wown, tall,
     local_sem, send_sem, recv_sem,
 ):
     nm, nl, mb, cl, cw, lv, mr, mw, fr, fw = dims
@@ -174,9 +179,7 @@
             wown[:, :, lanes] = moved[:, phase * LANES : (phase + 1) * LANES].reshape(fr, lp, LANES)
     w_up = lat_copy(6, 1, wown.at[pl.ds(fr - h2, h2)], wrows.at[0])
     w_dn = lat_copy(7, -1, wown.at[pl.ds(0, h2)], wrows.at[1])
-    for item in (w_up, w_dn):
-        start(item)
-        pending.append(item)
+    pending += [w_up, w_dn]
 
     wait_recv(c_up)
     wait_recv(c_dn)
@@ -186,43 +189,53 @@
     lon = lon_ref[...]
     wide = []
     for part in (below, own, above):
-        parts = split3(part.reshape(mb * cl, cw))
-        wide.append(dot(parts[0], lon) + (dot(parts[1], lon) + dot(parts[2], lon)))
+        parts = split2(part.reshape(mb * cl, cw))
+        wide.append(dot(parts[0], lon) + dot(parts[1], lon))
     cp_pert.wait()
-    up3 = up_ref[...]
+    def block_levels(b):
+        return pl.ds(8 * b, 8)
+
+    def mem_slice(device, b):
+        return pl.ds(pl.multiple_of(device * lp + 8 * b, 8), 8)
+
+    stacks = []
     for m in range(mb):
         stack = jnp.concatenate([w[m * cl : (m + 1) * cl] for w in wide], axis=0)
-        raised = dot(up3, jnp.concatenate(split3(stack), axis=0))
-        term = pert[m].astype(F32).reshape(lv * mr, mw) * raised
+        stacks.append(jnp.concatenate(split2(stack), axis=0))
+    part = lp * mr
+    rs = {}
+
+    def send_sum(b, k):
+        target = lax.rem(mem + k, nm)
+        slot = 10 + 6 * blocks + (b * nm + k)
+        copy = pltpu.make_async_remote_copy(
+            src_ref=mids.at[:, mem_slice(target, b), :],
+            dst_ref=rsr.at[k - 1, :, block_levels(b), :],
+            send_sem=send_sem.at[slot], recv_sem=recv_sem.at[slot],
+            device_id={"mem": target}, device_id_type=MESH,
+        )
+        copy.start()
+        rs[b, k] = copy
+
+    for k in list(range(1, nm)) + [0]:
+        target = lax.rem(mem + k, nm)
+        up2 = up_ref[pl.ds(pl.multiple_of(target * part, 16), part), :]
+        for m in range(mb):
+            raised = dot(up2, stacks[m])
+            level = pert[m, pl.ds(target * lp, lp)].astype(F32).reshape(part, mw)
+            total = level * raised if m == 0 else total + level * raised
         for t in range(qblocks):
-            piece = term[:, t * LANES : (t + 1) * LANES]
-            if m == 0:
-                ls[t] = piece
-            else:
-                ls[t] += piece
-    for r in range(mr):
-        for t in range(qblocks):
-            mids[r, :, t * LANES : (t + 1) * LANES] = ls[t, pl.ds(r, lv, stride=mr), :]
-
-    def block_levels(b):
-        return pl.ds(8 * b, 8)
-
-    def mem_slice(device, b):
-        return pl.ds(pl.multiple_of(device * lp + 8 * b, 8), 8)
-
-    rs = {}
-    for b in range(blocks):
+            ls[t, k * part : (k + 1) * part] = total[:, t * LANES : (t + 1) * LANES]
+        for r in range(mr):
+            for t in range(qblocks):
+                mids[
+                    r, pl.ds(pl.multiple_of(target * lp, 8), lp), t * LANES : (t + 1) * LANES
+                ] = ls[t, pl.ds(k * part + r, lp, stride=mr), :]
+        if k > 0:
+            send_sum(0, k)
+    for b in range(1, blocks):
         for k in range(1, nm):
-            target = lax.rem(mem + k, nm)
-            slot = 10 + 6 * blocks + (b * nm + k)
-            copy = pltpu.make_async_remote_copy(
-                src_ref=mids.at[:, mem_slice(target, b), :],
-                dst_ref=rsr.at[k - 1, :, block_levels(b), :],
-                send_sem=send_sem.at[slot], recv_sem=recv_sem.at[slot],
-                device_id={"mem": target}, device_id_type=MESH,
-            )
-            copy.start()
-            rs[b, k] = copy
+            send_sum(b, k)
 
     centre = 2 * mr
     zero_mid = jnp.zeros((mr, lp, mw), F32)
@@ -426,6 +439,8 @@
             ag[b, k] = copy
 
     near = {0: add_up(0)}
+    start(w_up)
+    start(w_dn)
     previous = None
     for b in range(blocks):
         if b == 0:
@@ -460,22 +475,32 @@
         smooth(b, PASSES)
         previous = transpose_rows(b)
     share(blocks - 1, previous)
-    for copy in ag.values():
-        copy.wait_recv()
-    for copy in rs.values():
-        copy.wait_send()
-    for r in range(mr):
-        for t in range(qblocks):
-            ls[t, pl.ds(r, lv, stride=mr), :] = fa[r, :, t * LANES : (t + 1) * LANES]
-    spread = jnp.concatenate([ls[t] for t in range(qblocks)], axis=1)
-
-    down = down_ref[...]
+    part = lp * mr
+    for k in range(nm):
+        source = lax.rem(mem + (nm - k), nm)
+        if k > 0:
+            for b in range(blocks):
+                ag[b, k].wait_recv()
+        for r in range(mr):
+            for t in range(qblocks):
+                ls[t, pl.ds(k * part + r, lp, stride=mr), :] = fa[
+                    r, pl.ds(pl.multiple_of(source * lp, 8), lp), t * LANES : (t + 1) * LANES
+                ]
+        spread = jnp.concatenate(
+            [ls[t, k * part : (k + 1) * part] for t in range(qblocks)], axis=1
+        )
+        down = down_ref[source]
+        for m in range(mb):
+            level = pert[m, pl.ds(source * lp, lp)].astype(F32).reshape(part, mw)
+            value = dot(down, jnp.concatenate(split2(level * spread), axis=0))
+            if k == 0:
+                tall[m] = value
+            else:
+                tall[m] += value
     lont = lont_ref[...]
     for m in range(mb):
-        parts = split3(pert[m].astype(F32).reshape(lv * mr, mw) * spread)
-        tall = dot(down, parts[0]) + (dot(down, parts[1]) + dot(down, parts[2]))
-        thin = split3(tall)
-        grad = dot(thin[0], lont) + (dot(thin[1], lont) + dot(thin[2], lont))
+        thin = split2(tall[m])
+        grad = dot(thin[0], lont) + dot(thin[1], lont)
         for c in range(3):
             gp[c, m] = grad[c * cl : (c + 1) * cl]
     g_up = lat_copy(8, 1, gp.at[2], gpr.at[0])
@@ -497,7 +522,7 @@
     out_ref[...] = ctl_ref[...] + (gp[1] + (gpr[0] + gpr[1]))
     for item in pending:
         wait_send(item)
-    for copy in ag.values():
+    for copy in list(rs.values()) + list(ag.values()):
         copy.wait_send()
 
 
@@ -512,6 +537,7 @@
     level = refine_matrix(cl, "edge")
     across = refine_matrix(1, "pad")
     up = np.einsum("vc,ra->vrac", level, across).reshape(lv * mr, 3 * cl)
+    down = up.T.reshape(3 * cl, nm, lp * mr).transpose(1, 0, 2)
     lon = refine_matrix(cw, "wrap").T
     vmem = pl.BlockSpec(memory_space=pltpu.VMEM)
     smem = pl.BlockSpec(memory_space=pltpu.SMEM)
@@ -544,6 +570,7 @@
             pltpu.VMEM((3, mb, cl, cw), F32),
             pltpu.VMEM((2, mb, cl, cw), F32),
             pltpu.VMEM((fr, lp, fw), F32),
+            pltpu.VMEM((mb, 3 * cl, mw), F32),
             pltpu.SemaphoreType.DMA((2,)),
             pltpu.SemaphoreType.DMA((slots,)),
             pltpu.SemaphoreType.DMA((slots,)),
@@ -557,9 +584,9 @@
         east_coef,
         fine_source,
         fine_frac,
-        jnp.asarray(np.concatenate([up] * 3, axis=1), BF16),
+        jnp.asarray(np.concatenate([up] * 2, axis=1), BF16),
         jnp.asarray(lon, BF16),
-        jnp.asarray(up.T, BF16),
+        jnp.asarray(np.concatenate([down] * 2, axis=2), BF16),
         jnp.asarray(lon.T, BF16),
     )
     return result.reshape(controls.shape)

time: 46 us -> 44.3 us (0.963); the launches traced: 45.8 us -> 43.6 us
  Pallas kernels: 44.4 us -> 42.2 us
    pallas_call x1, Pallas kernels: 44.4 us -> 42.2 us  [body(): pl.pallas_call(functools.partial(kernel, dims), out_shape=jax.ShapeDtypeS...]
where the time goes in v3:
time: 44.3 us; the launch traced here: 43.6 us
  Pallas kernels  42.2 us (95%)
  local copies, waits for them, and re-layouts  1.42 us (3%)
    pallas_call x1, Pallas kernels, body(): pl.pallas_call(functools.partial(kernel, dims), out_shape=jax.ShapeDtypeS...  42.2 us
    unnamed x1, local copies, waits for them, and re-layouts  1.42 us

profile of v3, /device:TPU:1, one launch (start us, length us, event | category | flops | bytes accessed | tf_op | source)
XLA Modules:
  0.0 43.6 jit_solution(12623550035531219350)
XLA Ops:
  0.0 42.2 %shard_map.109 = f32[6,16,96]{2,1,0:T(8,128)} custom-call(f32[6,16,96]{2,1,0:T(8,128)} %bitcast.5, bf16[6,64,4,384]{3,2,1,0:T(4,128)(2,1)} %pert_hbm.1, bf16[64,16,1536]{2,1,0:T(8,128)(2,1)} %pw_hbm.1, f32[16,1536]{1,0:T(8,128)} %north_ref.1, f32[16,1536]{1,0:T(8,128)} %east_ref.1, s32[16]{0:T(128)} %source_ref.1, f32[16]{0:T(128)} %frac_ref.1, ...), custom_call_target="tpu_custom_call" | custom-call | tf_op jit(solution)/shard_map/pallas_call | solution.py:549
  42.2 1.4 %copy.14 = f32[6,16,1,96]{3,2,1,0:T(1,128)} copy(f32[6,16,1,96]{3,2,1,0:T(1,128)} %bitcast.4) | data formatting | bytes 73728
